TPU v7x, 32 devices: a whole 2x2x4 slice. The times are simulated.
32 devices in a mesh: groups: 2 (over y), tm: 4 (over z), band: 2 (over x), tmpl: 2 (over core).
Axes of the slice: x: 2, y: 2, z: 4, core: 2. Of those that a mesh axis runs over, the one named last changes fastest.
Arguments:
- sft_bins: float32 [2, 128, 2048], P(None, ('groups', 'tm'), 'band'), parts along dimension 1, may hold values from -6 to 6
- delay_code: int32 [8, 128, 1024], P(('groups', 'tmpl'), None, ('tm', 'band')), parts along dimension 0, may hold values from 0 to 16007, as said below
- antenna: float32 [8, 2, 128, 1024], P(('groups', 'tmpl'), None, None, ('tm', 'band')), parts along dimension 0, may hold values from -10 to 10
Outputs:
- f_stat: float32 [8, 128, 8, 128], P(('groups', 'tmpl'), None, ('tm', 'band')), parts along dimension 0
There are 2 independent parts, one for each index of `groups`. A program takes and returns all parts, laid end to end along the dimension named above; each array names one. Nothing has to cross between parts.
Inputs may be any that keep to these rules, and one draw needn't show every extreme that they name: `delay_code`: the whole delay o of a template is the same for all samples n of each aligned run of 256 samples (n // 256 equal).
All inputs are finite; a program needn't handle non-finite values.
Results may differ from a plain program's by a relative error of at most 0.0003.
Values sent between devices are 32-bit elements; how exact they have to be, the bound alone decides.
No kernel may reach another device: no remote copies, remote signals or barrier semaphores. Data moves between devices by JAX's collectives and lax.ppermute only.
A program may use at most 64 MiB of HBM per device.

v0:
```python
import math
import jax
import jax.numpy as jnp
from jax import lax
from jax.sharding import PartitionSpec as P

NB = 2048
NQ = 128
NP = 16
SFT_DEV = 8
MAXD = 1000
NFRAC = 8
RUN = 256
stat_eps = 1e-06
floor_share = 0.5


def shifted(value, axis, by):
    length = lax.axis_size(axis)
    pairs = [(i, i + by) for i in range(length) if 0 <= i + by < length]
    return lax.ppermute(value, axis, pairs)


def lagrange(fraction):
    return (
        -fraction * (fraction - 1.0) * (fraction - 2.0) / 6.0,
        (fraction + 1.0) * (fraction - 1.0) * (fraction - 2.0) / 2.0,
        -(fraction + 1.0) * fraction * (fraction - 2.0) / 2.0,
        (fraction + 1.0) * fraction * (fraction - 1.0) / 6.0,
    )


def phase_pair(product, modulus, direction):
    angles = direction * 2.0 * math.pi / modulus * (product % modulus).astype(jnp.float32)
    return (jnp.cos(angles), jnp.sin(angles))


def dft_table(length, direction):
    rows_at = lax.broadcasted_iota(jnp.int32, (length, length), 0)
    cols_at = lax.broadcasted_iota(jnp.int32, (length, length), 1)
    return phase_pair(rows_at * cols_at, length, direction)


def complex_einsum(pattern, lhs_pair, rhs_pair):
    lhs_real, lhs_imag = lhs_pair
    rhs_real, rhs_imag = rhs_pair
    high = lax.Precision.HIGHEST
    out_real = jnp.einsum(pattern, lhs_real, rhs_real, precision=high) - jnp.einsum(
        pattern, lhs_imag, rhs_imag, precision=high
    )
    out_imag = jnp.einsum(pattern, lhs_real, rhs_imag, precision=high) + jnp.einsum(
        pattern, lhs_imag, rhs_real, precision=high
    )
    return (out_real, out_imag)


def rotate(values, phases):
    val_real, val_imag = values
    cos_part, sin_part = phases
    return (val_real * cos_part - val_imag * sin_part, val_real * sin_part + val_imag * cos_part)


def apply_weights(arrived):
    return arrived[:, 1][:, :, None] * arrived[:, 0][:, None]


def finish(arrived):
    owners = lax.axis_size("tm") * lax.axis_size("band")
    my_rank = lax.axis_index("tm") * lax.axis_size("band") + lax.axis_index("band")
    q_local = arrived.shape[3]
    lane_width = arrived.shape[5]
    sample_total = SFT_DEV * owners * NB
    section_one = complex_einsum(
        "abqix,ic->abqcx", (arrived[:, :, 0], arrived[:, :, 1]), dft_table(owners, -1.0)
    )
    c_pos = lax.broadcasted_iota(jnp.int32, (owners, lane_width), 0)
    x_pos = lax.broadcasted_iota(jnp.int32, (owners, lane_width), 1)
    section_one = rotate(section_one, phase_pair(c_pos * (x_pos // NP), SFT_DEV * owners, -1.0))
    short_table = dft_table(SFT_DEV, -1.0)
    ident_rows = jnp.eye(NP, dtype=jnp.float32)
    spread = (jnp.kron(short_table[0], ident_rows), jnp.kron(short_table[1], ident_rows))
    section_two = complex_einsum("abqcx,xy->abqcy", section_one, spread)
    q_grid = my_rank * q_local + lax.broadcasted_iota(jnp.int32, (q_local, owners, lane_width), 0)
    c_grid = lax.broadcasted_iota(jnp.int32, (q_local, owners, lane_width), 1)
    x_grid = lax.broadcasted_iota(jnp.int32, (q_local, owners, lane_width), 2)
    time_index = x_grid % NP + NP * q_grid
    freq_index = c_grid + owners * (x_grid // NP)
    section_two = rotate(section_two, phase_pair(time_index * freq_index, sample_total, -1.0))
    packed = jnp.stack(section_two, axis=2)
    turned = lax.all_to_all(packed, ("tm", "band"), split_axis=4, concat_axis=3, tiled=True)
    turned = turned.reshape(turned.shape[0], 2, 2, NQ, lane_width)
    section_three = complex_einsum(
        "abqx,qv->abvx", (turned[:, :, 0], turned[:, :, 1]), dft_table(NQ, -1.0)
    )
    v_pos = lax.broadcasted_iota(jnp.int32, (NQ, lane_width), 0)
    p_pos = lax.broadcasted_iota(jnp.int32, (NQ, lane_width), 1) % NP
    section_three = rotate(section_three, phase_pair(v_pos * p_pos, NB, -1.0))
    fine_table = dft_table(NP, -1.0)
    ident_blocks = jnp.eye(SFT_DEV, dtype=jnp.float32)
    block_table = (jnp.kron(ident_blocks, fine_table[0]), jnp.kron(ident_blocks, fine_table[1]))
    result = complex_einsum("abvx,xy->abvy", section_three, block_table)
    return jnp.stack(result, axis=2)


def per_device(sft_bins, delay_code, antenna):
    owners = lax.axis_size("tm") * lax.axis_size("band")
    sample_total = SFT_DEV * owners * NB
    spectra = lax.all_to_all(sft_bins, "band", split_axis=1, concat_axis=2, tiled=True)
    bin_grid = spectra.reshape(2, SFT_DEV, NP, NQ)
    section_one = complex_einsum("pk,skl->spl", dft_table(NP, 1.0), (bin_grid[0], bin_grid[1]))
    p_rows = lax.broadcasted_iota(jnp.int32, (NP, NQ), 0)
    l_cols = lax.broadcasted_iota(jnp.int32, (NP, NQ), 1)
    section_one = rotate(section_one, phase_pair(p_rows * l_cols, NB, 1.0))
    series_pair = complex_einsum("spl,lq->spq", section_one, dft_table(NQ, 1.0))
    norm_scale = 1.0 / math.sqrt(NB)
    stacked = jnp.stack([series_pair[0] * norm_scale, series_pair[1] * norm_scale])
    rim_cols = (MAXD + 1 + NP) // NP
    head_rim = stacked[:, 0, :, :rim_cols]
    tail_rim = stacked[:, SFT_DEV - 1, :, NQ - rim_cols :]
    after_rim = shifted(head_rim, ("tm", "band"), -1)
    before = shifted(tail_rim, ("tm", "band"), 1)
    rim_size = NP * rim_cols
    span_len = SFT_DEV * NB
    timed = stacked.transpose(0, 1, 3, 2).reshape(2, span_len)
    before_timed = before.transpose(0, 2, 1).reshape(2, rim_size)
    after_timed = after_rim.transpose(0, 2, 1).reshape(2, rim_size)
    buffer = jnp.concatenate([before_timed, timed, after_timed], axis=1)
    lane_width = SFT_DEV * NP
    tmpl_local = delay_code.shape[0]
    run_count = span_len // RUN
    code_time = (
        delay_code.reshape(tmpl_local, NQ, SFT_DEV, NP)
        .transpose(0, 2, 1, 3)
        .reshape(tmpl_local, run_count, RUN)
    )
    offsets = code_time[:, :, 0] // NFRAC - MAXD
    run_starts = (jnp.arange(run_count, dtype=jnp.int32) * RUN)[None, :] + offsets + (rim_size - 1)

    def take_segment(start):
        return lax.dynamic_slice_in_dim(buffer, start, RUN + 3, 1)

    segments = jax.vmap(jax.vmap(take_segment))(run_starts)
    fraction = (code_time % NFRAC).astype(jnp.float32) / NFRAC
    coeffs = lagrange(fraction)
    res_time = coeffs[0][:, :, None, :] * segments[:, :, :, 0:RUN]
    for tap_index in range(1, 4):
        res_time = (
            res_time
            + coeffs[tap_index][:, :, None, :] * segments[:, :, :, tap_index : tap_index + RUN]
        )
    resampled = res_time.transpose(0, 2, 1, 3).reshape(tmpl_local, 2, SFT_DEV, NQ, NP)
    resampled = resampled.transpose(0, 1, 3, 2, 4).reshape(tmpl_local, 2, NQ, lane_width)
    weight_a = antenna[:, 0]
    weight_b = antenna[:, 1]
    local_sums = jnp.stack(
        [
            jnp.sum(weight_a * weight_a, axis=(1, 2)),
            jnp.sum(weight_b * weight_b, axis=(1, 2)),
            jnp.sum(weight_a * weight_b, axis=(1, 2)),
        ],
        axis=1,
    )
    totals = lax.psum(local_sums, ("tm", "band"))
    payload = jnp.stack([resampled, antenna], axis=1)
    spectra_out = finish(
        apply_weights(
            lax.all_to_all(
                payload[:, :, :, :, None, :],
                ("tm", "band"),
                split_axis=3,
                concat_axis=4,
                tiled=True,
            )
        )
    )
    out_scale = 1.0 / math.sqrt(sample_total)
    a_real = spectra_out[:, 0, 0] * out_scale
    a_imag = spectra_out[:, 0, 1] * out_scale
    b_real = spectra_out[:, 1, 0] * out_scale
    b_imag = spectra_out[:, 1, 1] * out_scale
    power_a = (totals[:, 0] / sample_total + stat_eps)[:, None, None]
    power_b = (totals[:, 1] / sample_total + stat_eps)[:, None, None]
    cross_ab = (totals[:, 2] / sample_total)[:, None, None]
    det_floor = jnp.maximum(
        power_a * power_b - cross_ab * cross_ab, floor_share * power_a * power_b
    )
    f_stat = (
        power_b * (a_real * a_real + a_imag * a_imag)
        + power_a * (b_real * b_real + b_imag * b_imag)
        - 2.0 * cross_ab * (a_real * b_real + a_imag * b_imag)
    ) / det_floor
    return f_stat[:, :, None, :]


def solution(mesh):
    in_specs = (
        P(None, ("groups", "tm"), "band"),
        P(("groups", "tmpl"), None, ("tm", "band")),
        P(("groups", "tmpl"), None, None, ("tm", "band")),
    )
    out_specs = P(("groups", "tmpl"), None, ("tm", "band"), None)
    return jax.shard_map(
        per_device, mesh=mesh, in_specs=in_specs, out_specs=out_specs, check_vma=False
    )
```

profile of v0, /device:TPU:0, one launch (start us, length us, event | category | flops | bytes accessed | tf_op | source)
XLA Modules:
  0.0 251.6 jit_solution(13160571256986657289)
XLA Ops:
  0.0 1.7 copy.101
  1.7 4.2 %all-to-all-start = ((f32[2,16,1024]{2,0,1:T(2,128)}), f32[2,16,1024]{2,0,1:T(2,128)S(1)}, u32[]{:S(2)}, u32[]{:S(2)}) async-start(f32[2,16,1024]{2,0,1:T(2,128)} %copy.101), calls=%async_computation | async-start | bytes 262144 | tf_op jit(solution)/shard_map/all_to_all | solution.py:108
  6.1 1.8 copy.116
  7.9 1.1 multiply_reduce_fusion.2
  9.0 1.0 copy.99
  14.8 4.0 %collective-permute-start = (f32[2,16,63]{2,1,0:T(8,128)S(1)}, f32[2,16,63]{2,1,0:T(8,128)S(1)}, u32[]{:S(2)}, u32[]{:S(2)}) collective-permute-start(f32[2,16,63]{2,1,0:T(8,128)S(1)} %get-tuple-element.51), channel_id=1, source_target_pairs={{0,2},{2,4},{4,6},{6,8},{8,10},{10,12},{12,14},{1,3},{3,5},{5,7},{... | collective-permute-start | bytes 24200 | tf_op jit(solution)/shard_map/ppermute | solution.py:21
  18.8 1.3 collective-permute-start.1
  21.2 3.2 %collective-permute-done.1 = f32[2,16,63]{2,1,0:T(8,128)S(1)} collective-permute-done((f32[2,16,63]{2,1,0:T(8,128)S(1)}, f32[2,16,63]{2,1,0:T(8,128)S(1)}, u32[]{:S(2)}, u32[]{:S(2)}) %collective-permute-start.1) | collective-permute-done | bytes 8096 | tf_op jit(solution)/shard_map/ppermute | solution.py:21
  25.0 168.8 %while.1 = (s32[]{:T(128)}, f32[2,18400]{1,0:T(2,128)S(1)}, s32[128,2]{1,0:T(8,128)S(1)}, f32[128,2,259]{2,1,0:T(2,128)S(1)}, s32[]{:T(128)}) while((s32[]{:T(128)}, f32[2,18400]{1,0:T(2,128)S(1)}, s32[128,2]{1,0:T(8,128)S(1)}, f32[128,2,259]{2,1,0:T(2,128)S(1)}, s32[]{:T(128)}) %tuple.47), condition=%wide.while_cond, body=%wide.while_body.sunk | while | flops 2 | bytes 6241 | solution.py:140
  28.2 0.7 bitcast_dynamic-update-slice_fusion.2
  32.2 0.7 bitcast_dynamic-update-slice_fusion.2
  34.8 0.7 bitcast_dynamic-update-slice_fusion.2
  36.1 0.7 bitcast_dynamic-update-slice_fusion.2
  38.8 0.7 bitcast_dynamic-update-slice_fusion.2
  42.7 0.7 bitcast_dynamic-update-slice_fusion.2
  193.8 0.9 fusion.214
  196.0 1.0 maximum_bitcast_fusion
  197.0 1.0 copy.117
  198.0 5.8 %all-to-all-start.1 = ((f32[2,2,2,128,1,128]{5,2,0,1,4,3:T(2,128)}), f32[2,2,2,128,1,128]{5,2,0,1,4,3:T(2,128)S(1)}, u32[]{:S(2)}, u32[]{:S(2)}) async-start(f32[2,2,2,128,1,128]{5,2,0,1,4,3:T(2,128)} %copy.117), calls=%async_computation.1 | async-start | bytes 1048576 | tf_op jit(solution)/shard_map/all_to_all | solution.py:167
  203.8 22.1 %psum.7 = f32[2,3]{0,1:T(4,128)S(1)} all-reduce(f32[2,3]{0,1:T(4,128)S(1)} %pad_maximum_fusion.2), channel_id=1, replica_groups=mesh['groups'=2,'tm'=4,'band'=2,'tmpl'=2] {'tm','band'}, use_global_device_ids=true, to_apply=%region_3.4 | all-reduce | flops 6 | bytes 48 | tf_op jit(solution)/shard_map/psum | solution.py:163
  230.8 0.9 copy.123
  231.7 3.7 %all-to-all-start.2 = ((f32[2,2,2,16,8,128]{5,3,1,0,2,4:T(8,128)}), f32[2,2,2,16,8,128]{5,3,1,0,2,4:T(8,128)S(1)}, u32[]{:S(2)}, u32[]{:S(2)}) async-start(f32[2,2,2,16,8,128]{5,3,1,0,2,4:T(8,128)} %copy.123), calls=%async_computation.2 | async-start | bytes 1048576 | tf_op jit(solution)/shard_map/all_to_all | solution.py:90
  236.1 10.6 %all-to-all-done.2 = f32[2,2,2,16,8,128]{5,3,1,0,2,4:T(8,128)S(1)} async-done(((f32[2,2,2,16,8,128]{5,3,1,0,2,4:T(8,128)}), f32[2,2,2,16,8,128]{5,3,1,0,2,4:T(8,128)S(1)}, u32[]{:S(2)}, u32[]{:S(2)}) %all-to-all-start.2) | async-done | bytes 524320 | tf_op jit(solution)/shard_map/all_to_all | solution.py:90
  250.9 0.8 fusion.36
  (461 shorter events, 181.6 us)
Async XLA Ops:
  1.7 9.7 %all-to-all-start = ((f32[2,16,1024]{2,0,1:T(2,128)}), f32[2,16,1024]{2,0,1:T(2,128)S(1)}, u32[]{:S(2)}, u32[]{:S(2)}) async-start(f32[2,16,1024]{2,0,1:T(2,128)} %copy.101), calls=%async_computation | async-start | bytes 262144 | tf_op jit(solution)/shard_map/all_to_all | solution.py:108
  14.8 6.2 %collective-permute-start = (f32[2,16,63]{2,1,0:T(8,128)S(1)}, f32[2,16,63]{2,1,0:T(8,128)S(1)}, u32[]{:S(2)}, u32[]{:S(2)}) collective-permute-start(f32[2,16,63]{2,1,0:T(8,128)S(1)} %get-tuple-element.51), channel_id=1, source_target_pairs={{0,2},{2,4},{4,6},{6,8},{8,10},{10,12},{12,14},{1,3},{3,5},{5,7},{... | collective-permute-start | bytes 24200 | tf_op jit(solution)/shard_map/ppermute | solution.py:21
  18.8 5.6 %collective-permute-start.1 = (f32[2,16,63]{2,1,0:T(8,128)S(1)}, f32[2,16,63]{2,1,0:T(8,128)S(1)}, u32[]{:S(2)}, u32[]{:S(2)}) collective-permute-start(f32[2,16,63]{2,1,0:T(8,128)S(1)} %get-tuple-element.50), channel_id=1, source_target_pairs={{2,0},{4,2},{6,4},{8,6},{10,8},{12,10},{14,12},{3,1},{5,3},{7,5},{... | collective-permute-start | bytes 24200 | tf_op jit(solution)/shard_map/ppermute | solution.py:21
  198.0 29.2 %all-to-all-start.1 = ((f32[2,2,2,128,1,128]{5,2,0,1,4,3:T(2,128)}), f32[2,2,2,128,1,128]{5,2,0,1,4,3:T(2,128)S(1)}, u32[]{:S(2)}, u32[]{:S(2)}) async-start(f32[2,2,2,128,1,128]{5,2,0,1,4,3:T(2,128)} %copy.117), calls=%async_computation.1 | async-start | bytes 1048576 | tf_op jit(solution)/shard_map/all_to_all | solution.py:167
  231.7 15.0 %all-to-all-start.2 = ((f32[2,2,2,16,8,128]{5,3,1,0,2,4:T(8,128)}), f32[2,2,2,16,8,128]{5,3,1,0,2,4:T(8,128)S(1)}, u32[]{:S(2)}, u32[]{:S(2)}) async-start(f32[2,2,2,16,8,128]{5,3,1,0,2,4:T(8,128)} %copy.123), calls=%async_computation.2 | async-start | bytes 1048576 | tf_op jit(solution)/shard_map/all_to_all | solution.py:90
where the time goes:
time: 253 us; the launch traced here: 252 us
  local copies, waits for them, and re-layouts  181 us (72%)
  blocking collectives  22.1 us (9%)
  starting transfers between devices  19 us (8%)
  waiting for transfers between devices  13.8 us (5%)
  matrix products  10.2 us (4%)
  other arithmetic  4.66 us (2%)
    gather x384, local copies, waits for them, and re-layouts  169 us
    psum x1, blocking collectives, per_device(): totals = lax.psum(local_sums, ('tm', 'band'))  22.1 us
    all_to_all x1, waiting for transfers between devices, finish(): lax.all_to_all(packed, ('tm', 'band'), split_axis=4, concat_axis=3, tiled...  10.6 us
    all_to_all x1, starting transfers between devices, per_device(): lax.all_to_all(payload[:, :, :, :, None, :], ('tm', 'band'), split_axis=3...  5.76 us
    ppermute x2, starting transfers between devices, shifted(): return lax.ppermute(value, axis, pairs)  5.3 us
  transfers between devices with their start and end apart: 5, of which 2 were waited for; matrix products, arithmetic and copies ran while one was open for 3% of the time, Pallas kernels for 0%

commit v1 on v0

--- a/solution.py
+++ b/solution.py
@@ -87,7 +87,15 @@
     freq_index = c_grid + owners * (x_grid // NP)
     section_two = rotate(section_two, phase_pair(time_index * freq_index, sample_total, -1.0))
     packed = jnp.stack(section_two, axis=2)
-    turned = lax.all_to_all(packed, ("tm", "band"), split_axis=4, concat_axis=3, tiled=True)
+    turned = jnp.concatenate(
+        lax.all_to_all(
+            jnp.stack(jnp.split(packed, lax.axis_size(("tm", "band")), axis=4)),
+            ("tm", "band"),
+            0,
+            0,
+        ),
+        axis=3,
+    )
     turned = turned.reshape(turned.shape[0], 2, 2, NQ, lane_width)
     section_three = complex_einsum(
         "abqx,qv->abvx", (turned[:, :, 0], turned[:, :, 1]), dft_table(NQ, -1.0)

time: 253 us -> 258 us (1.020)
  local copies, waits for them, and re-layouts: 181 us -> 185 us
    unnamed x3 -> x10, local copies, waits for them, and re-layouts: 4.44 us -> 8.81 us
where the time goes in v1:
time: 258 us; the launch traced here: 256 us
  local copies, waits for them, and re-layouts  185 us (72%)
  blocking collectives  22.1 us (9%)
  starting transfers between devices  18.8 us (7%)
  waiting for transfers between devices  13.8 us (5%)
  matrix products  10.2 us (4%)
  other arithmetic  5.13 us (2%)
    gather x384, local copies, waits for them, and re-layouts  169 us
    psum x1, blocking collectives, per_device(): totals = lax.psum(local_sums, ('tm', 'band'))  22.1 us
    all_to_all x1, waiting for transfers between devices, finish(): lax.all_to_all(jnp.stack(jnp.split(packed, lax.axis_size(('tm', 'band')),...  10.6 us
    unnamed x10, local copies, waits for them, and re-layouts  8.81 us
    all_to_all x1, starting transfers between devices, per_device(): lax.all_to_all(payload[:, :, :, :, None, :], ('tm', 'band'), split_axis=3...  5.76 us
    ppermute x2, starting transfers between devices, shifted(): return lax.ppermute(value, axis, pairs)  5.31 us
  transfers between devices with their start and end apart: 5, of which 2 were waited for; matrix products, arithmetic and copies ran while one was open for 3% of the time, Pallas kernels for 0%

profile of v1, /device:TPU:0, one launch (start us, length us, event | category | flops | bytes accessed | tf_op | source)
XLA Modules:
  0.0 256.0 jit_solution(17080846605674349140)
XLA Ops:
  0.0 1.7 copy.122
  1.7 4.2 %all-to-all-start = ((f32[2,16,1024]{2,0,1:T(2,128)}), f32[2,16,1024]{2,0,1:T(2,128)S(1)}, u32[]{:S(2)}, u32[]{:S(2)}) async-start(f32[2,16,1024]{2,0,1:T(2,128)} %copy.122), calls=%async_computation | async-start | bytes 262144 | tf_op jit(solution)/shard_map/all_to_all | solution.py:116
  6.1 1.8 copy.137
  7.9 1.1 multiply_reduce_fusion.2
  9.0 1.0 copy.120
  14.8 4.0 %collective-permute-start = (f32[2,16,63]{2,1,0:T(8,128)S(1)}, f32[2,16,63]{2,1,0:T(8,128)S(1)}, u32[]{:S(2)}, u32[]{:S(2)}) collective-permute-start(f32[2,16,63]{2,1,0:T(8,128)S(1)} %get-tuple-element.59), channel_id=1, source_target_pairs={{0,2},{2,4},{4,6},{6,8},{8,10},{10,12},{12,14},{1,3},{3,5},{5,7},{... | collective-permute-start | bytes 24200 | tf_op jit(solution)/shard_map/ppermute | solution.py:21
  18.8 1.3 collective-permute-start.1
  21.2 3.2 %collective-permute-done.1 = f32[2,16,63]{2,1,0:T(8,128)S(1)} collective-permute-done((f32[2,16,63]{2,1,0:T(8,128)S(1)}, f32[2,16,63]{2,1,0:T(8,128)S(1)}, u32[]{:S(2)}, u32[]{:S(2)}) %collective-permute-start.1) | collective-permute-done | bytes 8096 | tf_op jit(solution)/shard_map/ppermute | solution.py:21
  25.0 168.8 %while.1 = (s32[]{:T(128)}, f32[2,18400]{1,0:T(2,128)S(1)}, s32[128,2]{1,0:T(8,128)S(1)}, f32[128,2,259]{2,1,0:T(2,128)S(1)}, s32[]{:T(128)}) while((s32[]{:T(128)}, f32[2,18400]{1,0:T(2,128)S(1)}, s32[128,2]{1,0:T(8,128)S(1)}, f32[128,2,259]{2,1,0:T(2,128)S(1)}, s32[]{:T(128)}) %tuple.54), condition=%wide.while_cond, body=%wide.while_body.sunk | while | flops 2 | bytes 6241 | solution.py:148
  28.2 0.7 bitcast_dynamic-update-slice_fusion.2
  32.2 0.7 bitcast_dynamic-update-slice_fusion.2
  34.8 0.7 bitcast_dynamic-update-slice_fusion.2
  38.8 0.7 bitcast_dynamic-update-slice_fusion.2
  42.7 0.7 bitcast_dynamic-update-slice_fusion.2
  45.4 0.7 bitcast_dynamic-update-slice_fusion.2
  46.7 0.7 bitcast_dynamic-update-slice_fusion.2
  193.8 0.9 fusion.221
  196.0 1.0 maximum_bitcast_fusion
  197.0 1.0 copy.138
  198.0 5.8 %all-to-all-start.1 = ((f32[2,2,2,128,1,128]{5,2,0,1,4,3:T(2,128)}), f32[2,2,2,128,1,128]{5,2,0,1,4,3:T(2,128)S(1)}, u32[]{:S(2)}, u32[]{:S(2)}) async-start(f32[2,2,2,128,1,128]{5,2,0,1,4,3:T(2,128)} %copy.138), calls=%async_computation.1 | async-start | bytes 1048576 | tf_op jit(solution)/shard_map/all_to_all | solution.py:175
  203.8 22.1 %psum.7 = f32[2,3]{0,1:T(4,128)S(1)} all-reduce(f32[2,3]{0,1:T(4,128)S(1)} %pad_maximum_fusion.2), channel_id=1, replica_groups=mesh['groups'=2,'tm'=4,'band'=2,'tmpl'=2] {'tm','band'}, use_global_device_ids=true, to_apply=%region_3.4 | all-reduce | flops 6 | bytes 48 | tf_op jit(solution)/shard_map/psum | solution.py:171
  236.3 3.5 %all-to-all-start.2 = ((f32[8,2,2,2,16,1,128]{6,4,2,1,3,5,0:T(8,128)}), f32[8,2,2,2,16,1,128]{6,4,2,1,3,5,0:T(8,128)S(1)}, u32[]{:S(2)}, u32[]{:S(2)}) async-start(f32[8,2,2,2,16,1,128]{6,4,2,1,3,5,0:T(8,128)} %constant_dynamic-update-slice_fusion), calls=%async_computation.2 | async-start | bytes 1048576 | tf_op jit(solution)/shard_map/all_to_all | solution.py:91
  240.5 10.6 %all-to-all-done.2 = f32[8,2,2,2,16,1,128]{6,4,2,1,3,5,0:T(8,128)S(1)} async-done(((f32[8,2,2,2,16,1,128]{6,4,2,1,3,5,0:T(8,128)}), f32[8,2,2,2,16,1,128]{6,4,2,1,3,5,0:T(8,128)S(1)}, u32[]{:S(2)}, u32[]{:S(2)}) %all-to-all-start.2) | async-done | bytes 524320 | tf_op jit(solution)/shard_map/all_to_all | solution.py:91
  255.2 0.8 fusion.36
  (468 shorter events, 186.3 us)
Async XLA Ops:
  1.7 9.7 %all-to-all-start = ((f32[2,16,1024]{2,0,1:T(2,128)}), f32[2,16,1024]{2,0,1:T(2,128)S(1)}, u32[]{:S(2)}, u32[]{:S(2)}) async-start(f32[2,16,1024]{2,0,1:T(2,128)} %copy.122), calls=%async_computation | async-start | bytes 262144 | tf_op jit(solution)/shard_map/all_to_all | solution.py:116
  14.8 6.2 %collective-permute-start = (f32[2,16,63]{2,1,0:T(8,128)S(1)}, f32[2,16,63]{2,1,0:T(8,128)S(1)}, u32[]{:S(2)}, u32[]{:S(2)}) collective-permute-start(f32[2,16,63]{2,1,0:T(8,128)S(1)} %get-tuple-element.59), channel_id=1, source_target_pairs={{0,2},{2,4},{4,6},{6,8},{8,10},{10,12},{12,14},{1,3},{3,5},{5,7},{... | collective-permute-start | bytes 24200 | tf_op jit(solution)/shard_map/ppermute | solution.py:21
  18.8 5.6 %collective-permute-start.1 = (f32[2,16,63]{2,1,0:T(8,128)S(1)}, f32[2,16,63]{2,1,0:T(8,128)S(1)}, u32[]{:S(2)}, u32[]{:S(2)}) collective-permute-start(f32[2,16,63]{2,1,0:T(8,128)S(1)} %get-tuple-element.58), channel_id=1, source_target_pairs={{2,0},{4,2},{6,4},{8,6},{10,8},{12,10},{14,12},{3,1},{5,3},{7,5},{... | collective-permute-start | bytes 24200 | tf_op jit(solution)/shard_map/ppermute | solution.py:21
  198.0 29.2 %all-to-all-start.1 = ((f32[2,2,2,128,1,128]{5,2,0,1,4,3:T(2,128)}), f32[2,2,2,128,1,128]{5,2,0,1,4,3:T(2,128)S(1)}, u32[]{:S(2)}, u32[]{:S(2)}) async-start(f32[2,2,2,128,1,128]{5,2,0,1,4,3:T(2,128)} %copy.138), calls=%async_computation.1 | async-start | bytes 1048576 | tf_op jit(solution)/shard_map/all_to_all | solution.py:175
  236.3 14.8 %all-to-all-start.2 = ((f32[8,2,2,2,16,1,128]{6,4,2,1,3,5,0:T(8,128)}), f32[8,2,2,2,16,1,128]{6,4,2,1,3,5,0:T(8,128)S(1)}, u32[]{:S(2)}, u32[]{:S(2)}) async-start(f32[8,2,2,2,16,1,128]{6,4,2,1,3,5,0:T(8,128)} %constant_dynamic-update-slice_fusion), calls=%async_computation.2 | async-start | bytes 1048576 | tf_op jit(solution)/shard_map/all_to_all | solution.py:91
